TPU v7x, 32 devices: a whole 2x2x4 slice. The times are simulated.
32 devices in a mesh: layer: 4 (over z), row: 2 (over x), col: 4 (over y, core).
Axes of the slice: x: 2, y: 2, z: 4, core: 2. Of those that a mesh axis runs over, the one named last changes fastest.
Arguments:
- cost_vector: float32 [8, 1024, 512], P('layer', 'row', 'col'), may hold values from -12 to 12
- metal_density: float32 [8, 1024, 512], P('layer', 'row', 'col'), may hold values from 0 to 0.5
- cap_class: int32 [8, 1024, 512], P('layer', 'row', 'col'), may hold values from 0 to 7
- blocked_mask: int32 [8, 1024, 512], P('layer', 'row', 'col'), may hold values 0 or 1
- fill_start: float32 [8, 1024, 512], P('layer', 'row', 'col'), may hold values from 0 to 1
- window_dual: float32 [8, 1024, 512], P('layer', 'row', 'col'), may hold values from -4 to 4
- layer_dual: float32 [8, 1024, 512], P('layer', 'row', 'col'), may hold values from -4 to 4
Outputs:
- fill_level: float32 [8, 1024, 512], P('layer', 'row', 'col')
- window_price: float32 [8, 1024, 512], P('layer', 'row', 'col')
- layer_price: float32 [8, 1024, 512], P('layer', 'row', 'col')
- primal_weight: float32 [], replicated
All inputs are finite; a program needn't handle non-finite values. No bound on the sum of `blocked_mask` on one device may be relied on, other than what follows from the above.
Results may differ from a plain program's by a relative error of at most 0.00011.
Values sent between devices are 32-bit elements; how exact they have to be, the bound alone decides.
A program may use at most 64 MiB of HBM per device.

v0:
```python
import jax
import jax.numpy as jnp
from jax import lax
from jax.sharding import PartitionSpec as P

WIN = 50
CAP_LEVELS = 8
ITERS = 3
step_eta = 0.4
low_density = 0.35
high_density = 0.65
layer_gap = 0.15
tiny_term = 1e-06


def extended(cells, sides, width):
    for axis, dim in sides:
        count = lax.axis_size(axis)
        ends = count - 1
        head = lax.slice_in_dim(cells, 0, width, axis=dim)
        tail = lax.slice_in_dim(cells, cells.shape[dim] - width, cells.shape[dim], axis=dim)
        cells = jnp.concatenate(
            [
                lax.ppermute(tail, axis, [(i, (i + 1) % count) for i in range(ends)]),
                cells,
                lax.ppermute(head, axis, [((i + 1) % count, i) for i in range(ends)]),
            ],
            axis=dim,
        )
    return cells


def from_behind(block, axis, distance):
    devices = range(lax.axis_size(axis))
    route = [(i - distance, i) for i in devices if i - distance in devices]
    return lax.ppermute(block, axis, route)


def band_matrix(extent_out, extent_in, offset):
    index_out = lax.broadcasted_iota(jnp.int32, (extent_out, extent_in), 0)
    index_in = lax.broadcasted_iota(jnp.int32, (extent_out, extent_in), 1)
    spread = index_in - index_out
    return ((spread >= offset) & (spread < offset + WIN)).astype(jnp.float32)


def rows_pass(row_band, padded):
    return jnp.einsum("ip,lpq->liq", row_band, padded, precision=lax.Precision.HIGHEST)


def cols_pass(partial_sum, col_band):
    return jnp.einsum("liq,qj->lij", partial_sum, col_band, precision=lax.Precision.HIGHEST)


def fill_window(level, row_band, col_band, halfway):
    tall = extended(level, (("row", 1),), halfway)
    partial_sum = rows_pass(row_band, tall)
    wide = extended(partial_sum, (("col", 2),), halfway)
    result = cols_pass(wide, col_band)
    return result


def dual_window(density_dual, row_band, col_band, halfway):
    tall = extended(density_dual, (("row", 1),), halfway)
    partial_sum = rows_pass(row_band, tall)
    wide = extended(partial_sum, (("col", 2),), halfway)
    result = cols_pass(wide, col_band)
    return result


def local(cost_vector, metal_density, cap_class, blocked_mask, fill_start, window_dual, layer_dual):
    layers_here, row_count, col_count = fill_start.shape
    halfway = WIN // 2
    inverse_area = 1.0 / (WIN * WIN)
    row_forward = band_matrix(row_count, row_count + 2 * halfway, 0)
    row_backward = band_matrix(row_count, row_count + 2 * halfway, 1)
    col_forward = band_matrix(col_count, col_count + 2 * halfway, 0).T
    col_backward = band_matrix(col_count, col_count + 2 * halfway, 1).T
    layer_ids = lax.axis_index("layer") * layers_here + lax.iota(jnp.int32, layers_here)
    keep_mask = (layer_ids < lax.axis_size("layer") * layers_here - 1).astype(jnp.float32)[
        :, None, None
    ]
    capacity = jnp.where(blocked_mask == 1, 0.0, (cap_class + 1).astype(jnp.float32) / CAP_LEVELS)
    has_floor = blocked_mask == 0
    filling = fill_start
    density_dual = window_dual
    stacked_dual = layer_dual * keep_mask
    weight = jnp.float32(1.0)
    for iteration in range(ITERS):
        primal_step = step_eta / weight
        dual_step = step_eta * weight
        below = from_behind(stacked_dual[layers_here - 1 :], "layer", 1)
        earlier = jnp.concatenate([below, stacked_dual[: layers_here - 1]], axis=0)
        transposed = dual_window(density_dual, row_backward, col_backward, halfway)
        gradient = cost_vector + transposed * inverse_area + (stacked_dual - earlier)
        fill_new = jnp.clip(filling - primal_step * gradient, 0.0, capacity)
        moved = fill_new - filling
        primal_sum = jnp.sum(moved * moved)
        level = fill_new + moved + metal_density
        above = from_behind(level[0:1], "layer", -1)
        later = jnp.concatenate([level[1:], above], axis=0)
        forward = fill_window(level, row_forward, col_forward, halfway)
        window_term = density_dual / dual_step + forward * inverse_area
        capped = jnp.minimum(window_term, high_density)
        clipped = jnp.where(has_floor, jnp.maximum(capped, low_density), capped)
        density_new = dual_step * (window_term - clipped)
        layer_term = stacked_dual / dual_step + keep_mask * (level - later)
        stacked_new = (
            dual_step * (layer_term - jnp.clip(layer_term, -layer_gap, layer_gap)) * keep_mask
        )
        density_move = density_new - density_dual
        stacked_move = stacked_new - stacked_dual
        dual_sum = jnp.sum(density_move * density_move) + jnp.sum(stacked_move * stacked_move)
        primal_sum, dual_sum = lax.psum((primal_sum, dual_sum), ("layer", "row", "col"))
        weight = jnp.sqrt(weight) * jnp.sqrt(
            jnp.sqrt((dual_sum + tiny_term) / (primal_sum + tiny_term))
        )
        filling = fill_new
        density_dual = density_new
        stacked_dual = stacked_new
    return (filling, density_dual, stacked_dual, weight)


def solution(mesh):
    in_specs = (
        P("layer", "row", "col"),
        P("layer", "row", "col"),
        P("layer", "row", "col"),
        P("layer", "row", "col"),
        P("layer", "row", "col"),
        P("layer", "row", "col"),
        P("layer", "row", "col"),
    )
    out_specs = (P("layer", "row", "col"), P("layer", "row", "col"), P("layer", "row", "col"), P())
    return jax.shard_map(local, mesh=mesh, in_specs=in_specs, out_specs=out_specs, check_vma=False)
```

profile of v0, /device:TPU:0, one launch (start us, length us, event | category | flops | bytes accessed | tf_op | source)
XLA Modules:
  0.0 268.0 jit_solution(12571616555059935040)
XLA Ops:
  1.4 4.9 %collective-permute-start = (f32[2,25,128]{2,1,0:T(8,128)S(1)}, f32[2,25,128]{2,1,0:T(8,128)S(1)}, u32[]{:S(2)}, u32[]{:S(2)}) collective-permute-start(f32[2,25,128]{2,1,0:T(8,128)S(1)} %get-tuple-element.56), channel_id=1, source_target_pairs={{0,4},{1,5},{2,6},{3,7},{8,12},{9,13},{10,14},{11,15},{16,20},{17,... | collective-permute-start | bytes 76808 | tf_op jit(solution)/shard_map/ppermute | solution.py:24
  6.3 1.3 collective-permute-start.1
  8.8 3.6 %collective-permute-start.4 = (f32[1,512,128]{2,1,0:T(8,128)S(1)}, f32[1,512,128]{2,1,0:T(8,128)S(1)}, u32[]{:S(2)}, u32[]{:S(2)}) collective-permute-start(f32[1,512,128]{2,1,0:T(8,128)S(1)} %get-tuple-element.52), channel_id=1, source_target_pairs={{0,8},{8,16},{16,24},{1,9},{9,17},{17,25},{2,10},{10,18},{18,26},{... | collective-permute-start | bytes 786440 | tf_op jit(solution)/shard_map/ppermute | solution.py:36
  13.5 1.4 collective-permute-start.2
  14.9 1.3 collective-permute-start.3
  16.2 3.7 %collective-permute-done.3 = f32[2,512,25]{1,2,0:T(8,128)S(1)} collective-permute-done((f32[2,512,25]{1,2,0:T(8,128)S(1)}, f32[2,512,25]{1,2,0:T(8,128)S(1)}, u32[]{:S(2)}, u32[]{:S(2)}) %collective-permute-start.3) | collective-permute-done | bytes 102432 | tf_op jit(solution)/shard_map/ppermute | solution.py:26
  20.0 2.5 multiply_reduce_fusion.6
  22.5 4.5 %collective-permute-start.5 = (f32[2,25,128]{2,1,0:T(8,128)S(1)}, f32[2,25,128]{2,1,0:T(8,128)S(1)}, u32[]{:S(2)}, u32[]{:S(2)}) collective-permute-start(f32[2,25,128]{2,1,0:T(8,128)S(1)} %get-tuple-element.50), channel_id=1, source_target_pairs={{0,4},{1,5},{2,6},{3,7},{8,12},{9,13},{10,14},{11,15},{16,20},{17,... | collective-permute-start | bytes 76808 | tf_op jit(solution)/shard_map/ppermute | solution.py:24
  27.0 1.3 collective-permute-start.6
  28.6 4.2 %collective-permute-done.6 = f32[2,25,128]{2,1,0:T(8,128)S(1)} collective-permute-done((f32[2,25,128]{2,1,0:T(8,128)S(1)}, f32[2,25,128]{2,1,0:T(8,128)S(1)}, u32[]{:S(2)}, u32[]{:S(2)}) %collective-permute-start.6) | collective-permute-done | bytes 25632 | tf_op jit(solution)/shard_map/ppermute | solution.py:26
  33.8 4.0 %collective-permute-start.7 = (f32[2,512,25]{1,2,0:T(8,128)S(1)}, f32[2,512,25]{1,2,0:T(8,128)S(1)}, u32[]{:S(2)}, u32[]{:S(2)}) collective-permute-start(f32[2,512,25]{1,2,0:T(8,128)S(1)} %get-tuple-element.48), channel_id=1, source_target_pairs={{0,1},{1,2},{2,3},{4,5},{5,6},{6,7},{8,9},{9,10},{10,11},{12,13},{... | collective-permute-start | bytes 307208 | tf_op jit(solution)/shard_map/ppermute | solution.py:24
  37.8 1.3 collective-permute-start.8
  39.2 1.3 collective-permute-start.9
  40.5 1.4 collective-permute-done.8
  41.9 1.7 multiply_reduce_fusion.8
  43.6 1.6 collective-permute-start.10
  45.2 1.3 collective-permute-start.11
  46.8 4.2 %collective-permute-done.11 = f32[2,25,128]{2,1,0:T(8,128)S(1)} collective-permute-done((f32[2,25,128]{2,1,0:T(8,128)S(1)}, f32[2,25,128]{2,1,0:T(8,128)S(1)}, u32[]{:S(2)}, u32[]{:S(2)}) %collective-permute-start.11) | collective-permute-done | bytes 25632 | tf_op jit(solution)/shard_map/ppermute | solution.py:26
  52.9 3.5 %collective-permute-start.14 = (f32[1,512,128]{2,1,0:T(8,128)S(1)}, f32[1,512,128]{2,1,0:T(8,128)S(1)}, u32[]{:S(2)}, u32[]{:S(2)}) collective-permute-start(f32[1,512,128]{2,1,0:T(8,128)S(1)} %get-tuple-element.40), channel_id=1, source_target_pairs={{0,8},{8,16},{16,24},{1,9},{9,17},{17,25},{2,10},{10,18},{18,26},{... | collective-permute-start | bytes 786440 | tf_op jit(solution)/shard_map/ppermute | solution.py:36
  57.2 4.7 %collective-permute-start.12 = (f32[2,512,25]{1,2,0:T(8,128)}, f32[2,512,25]{1,2,0:T(8,128)}, u32[]{:S(2)}, u32[]{:S(2)}) collective-permute-start(f32[2,512,25]{1,2,0:T(8,128)} %get-tuple-element.44), channel_id=1, source_target_pairs={{0,1},{1,2},{2,3},{4,5},{5,6},{6,7},{8,9},{9,10},{10,11},{12,13},{... | collective-permute-start | bytes 307208 | tf_op jit(solution)/shard_map/ppermute | solution.py:24
  64.4 40.6 %all-reduce.2 = (f32[]{:T(128)}, f32[]{:T(128)}) all-reduce(f32[]{:T(128)S(6)} %add.115, f32[]{:T(128)} %get-tuple-element.20), channel_id=1, replica_groups=mesh['layer'=4,'row'=2,'col'=4] {'layer','row','col'}, use_global_device_ids=true, to_apply=%region_2.3 | all-reduce | flops 2 | bytes 16 | tf_op jit(solution)/shard_map/psum | solution.py:113
  107.2 3.9 %multiply_reduce_fusion.3 = (f32[]{:T(128)}, f32[2,512,128]{2,1,0:T(8,128)S(1)}, f32[2,512,128]{2,1,0:T(8,128)}) fusion(f32[2,512,128]{2,1,0:T(8,128)} %get-tuple-element.58, f32[2,512,128]{2,1,0:T(8,128)S(1)} %copy-done.1, f32[2,512,128]{2,1,0:T(8,128)S(1)} %get-tuple-element.15, f32[1,512,128]{2,1,0:T(8,128)S(1)} %get-tuple-element.41, ...), kind=kOutput, calls=%fused_computation.139 | convolution fusion | flops 282915840 | bytes 5447688 | tf_op jit(solution)/shard_map/liq,qj->lij/dot_general | solution.py:51
  111.1 4.2 %collective-permute-start.15 = (f32[2,25,128]{2,1,0:T(8,128)S(1)}, f32[2,25,128]{2,1,0:T(8,128)S(1)}, u32[]{:S(2)}, u32[]{:S(2)}) collective-permute-start(f32[2,25,128]{2,1,0:T(8,128)S(1)} %get-tuple-element.38), channel_id=1, source_target_pairs={{0,4},{1,5},{2,6},{3,7},{8,12},{9,13},{10,14},{11,15},{16,20},{17,... | collective-permute-start | bytes 76808 | tf_op jit(solution)/shard_map/ppermute | solution.py:24
  115.2 1.3 collective-permute-start.16
  116.8 4.2 %collective-permute-done.16 = f32[2,25,128]{2,1,0:T(8,128)S(1)} collective-permute-done((f32[2,25,128]{2,1,0:T(8,128)S(1)}, f32[2,25,128]{2,1,0:T(8,128)S(1)}, u32[]{:S(2)}, u32[]{:S(2)}) %collective-permute-start.16) | collective-permute-done | bytes 25632 | tf_op jit(solution)/shard_map/ppermute | solution.py:26
  122.0 1.3 collective-permute-start.17
  123.3 1.4 collective-permute-start.18
  124.8 1.3 collective-permute-start.19
  126.1 2.9 %collective-permute-done.18 = f32[2,512,25]{1,2,0:T(8,128)S(1)} collective-permute-done((f32[2,512,25]{1,2,0:T(8,128)S(1)}, f32[2,512,25]{1,2,0:T(8,128)S(1)}, u32[]{:S(2)}, u32[]{:S(2)}) %collective-permute-start.18) | collective-permute-done | bytes 102432 | tf_op jit(solution)/shard_map/ppermute | solution.py:26
  129.0 1.7 multiply_reduce_fusion.5
  130.8 1.6 collective-permute-start.20
  132.4 1.5 collective-permute-start.21
  134.0 4.2 %collective-permute-done.21 = f32[2,25,128]{2,1,0:T(8,128)S(1)} collective-permute-done((f32[2,25,128]{2,1,0:T(8,128)S(1)}, f32[2,25,128]{2,1,0:T(8,128)S(1)}, u32[]{:S(2)}, u32[]{:S(2)}) %collective-permute-start.21) | collective-permute-done | bytes 25632 | tf_op jit(solution)/shard_map/ppermute | solution.py:26
  140.2 2.4 collective-permute-start.24
  143.3 4.7 %collective-permute-start.22 = (f32[2,512,25]{1,2,0:T(8,128)}, f32[2,512,25]{1,2,0:T(8,128)}, u32[]{:S(2)}, u32[]{:S(2)}) collective-permute-start(f32[2,512,25]{1,2,0:T(8,128)} %get-tuple-element.32), channel_id=1, source_target_pairs={{0,1},{1,2},{2,3},{4,5},{5,6},{6,7},{8,9},{9,10},{10,11},{12,13},{... | collective-permute-start | bytes 307208 | tf_op jit(solution)/shard_map/ppermute | solution.py:24
  150.6 40.6 %all-reduce.1 = (f32[]{:T(128)}, f32[]{:T(128)}) all-reduce(f32[]{:T(128)S(6)} %add.124, f32[]{:T(128)} %get-tuple-element.18), channel_id=1, replica_groups=mesh['layer'=4,'row'=2,'col'=4] {'layer','row','col'}, use_global_device_ids=true, to_apply=%region_7.8 | all-reduce | flops 2 | bytes 16 | tf_op jit(solution)/shard_map/psum | solution.py:113
  193.4 3.9 %multiply_reduce_fusion = (f32[]{:T(128)}, f32[2,512,128]{2,1,0:T(8,128)S(1)}, f32[2,512,128]{2,1,0:T(8,128)}) fusion(f32[2,512,128]{2,1,0:T(8,128)} %get-tuple-element.61, f32[2,512,128]{2,1,0:T(8,128)S(1)} %copy-done.1, f32[2,512,128]{2,1,0:T(8,128)S(1)} %get-tuple-element.13, f32[1,512,128]{2,1,0:T(8,128)S(1)} %get-tuple-element.29, ...), kind=kOutput, calls=%fused_computation.134 | convolution fusion | flops 282915840 | bytes 5447688 | tf_op jit(solution)/shard_map/liq,qj->lij/dot_general | solution.py:51
  197.3 4.2 %collective-permute-start.25 = (f32[2,25,128]{2,1,0:T(8,128)S(1)}, f32[2,25,128]{2,1,0:T(8,128)S(1)}, u32[]{:S(2)}, u32[]{:S(2)}) collective-permute-start(f32[2,25,128]{2,1,0:T(8,128)S(1)} %get-tuple-element.26), channel_id=1, source_target_pairs={{0,4},{1,5},{2,6},{3,7},{8,12},{9,13},{10,14},{11,15},{16,20},{17,... | collective-permute-start | bytes 76808 | tf_op jit(solution)/shard_map/ppermute | solution.py:24
  201.5 1.3 collective-permute-start.26
  203.1 4.2 %collective-permute-done.26 = f32[2,25,128]{2,1,0:T(8,128)S(1)} collective-permute-done((f32[2,25,128]{2,1,0:T(8,128)S(1)}, f32[2,25,128]{2,1,0:T(8,128)S(1)}, u32[]{:S(2)}, u32[]{:S(2)}) %collective-permute-start.26) | collective-permute-done | bytes 25632 | tf_op jit(solution)/shard_map/ppermute | solution.py:26
  208.2 1.3 collective-permute-start.27
  209.5 1.4 collective-permute-start.28
  211.0 1.3 collective-permute-start.29
  212.4 2.9 %collective-permute-done.28 = f32[2,512,25]{1,2,0:T(8,128)S(1)} collective-permute-done((f32[2,512,25]{1,2,0:T(8,128)S(1)}, f32[2,512,25]{1,2,0:T(8,128)S(1)}, u32[]{:S(2)}, u32[]{:S(2)}) %collective-permute-start.28) | collective-permute-done | bytes 102432 | tf_op jit(solution)/shard_map/ppermute | solution.py:26
  215.3 2.5 multiply_reduce_fusion.2
  217.8 1.8 collective-permute-done.29
  219.6 1.7 multiply_reduce_fusion.1
  222.5 43.0 %all-reduce = (f32[]{:T(128)}, f32[]{:T(128)}) all-reduce(f32[]{:T(128)S(6)} %add.133, f32[]{:T(128)} %get-tuple-element.16), channel_id=1, replica_groups=mesh['layer'=4,'row'=2,'col'=4] {'layer','row','col'}, use_global_device_ids=true, to_apply=%region_12.13 | all-reduce | flops 2 | bytes 16 | tf_op jit(solution)/shard_map/psum | solution.py:113
  (84 shorter events, 16.3 us)
Async XLA Ops:
  1.4 11.0 %collective-permute-start = (f32[2,25,128]{2,1,0:T(8,128)S(1)}, f32[2,25,128]{2,1,0:T(8,128)S(1)}, u32[]{:S(2)}, u32[]{:S(2)}) collective-permute-start(f32[2,25,128]{2,1,0:T(8,128)S(1)} %get-tuple-element.56), channel_id=1, source_target_pairs={{0,4},{1,5},{2,6},{3,7},{8,12},{9,13},{10,14},{11,15},{16,20},{17,... | collective-permute-start | bytes 76808 | tf_op jit(solution)/shard_map/ppermute | solution.py:24
  6.3 6.2 %collective-permute-start.1 = (f32[2,25,128]{2,1,0:T(8,128)S(1)}, f32[2,25,128]{2,1,0:T(8,128)S(1)}, u32[]{:S(2)}, u32[]{:S(2)}) collective-permute-start(f32[2,25,128]{2,1,0:T(8,128)S(1)} %get-tuple-element.57), channel_id=1, source_target_pairs={{4,0},{5,1},{6,2},{7,3},{12,8},{13,9},{14,10},{15,11},{20,16},{21,... | collective-permute-start | bytes 76808 | tf_op jit(solution)/shard_map/ppermute | solution.py:26
  8.8 3.7 %copy-start.11 = (f32[2,512,128]{2,1,0:T(8,128)S(1)}, f32[2,512,128]{2,1,0:T(8,128)}, u32[]{:S(2)}) copy-start(f32[2,512,128]{2,1,0:T(8,128)} %param.12) | copy-start | bytes 1572868
  8.8 11.1 %collective-permute-start.4 = (f32[1,512,128]{2,1,0:T(8,128)S(1)}, f32[1,512,128]{2,1,0:T(8,128)S(1)}, u32[]{:S(2)}, u32[]{:S(2)}) collective-permute-start(f32[1,512,128]{2,1,0:T(8,128)S(1)} %get-tuple-element.52), channel_id=1, source_target_pairs={{0,8},{8,16},{16,24},{1,9},{9,17},{17,25},{2,10},{10,18},{18,26},{... | collective-permute-start | bytes 786440 | tf_op jit(solution)/shard_map/ppermute | solution.py:36
  12.5 7.4 %copy-start.1 = (f32[2,512,128]{2,1,0:T(8,128)S(1)}, f32[2,512,128]{2,1,0:T(8,128)}, u32[]{:S(2)}) copy-start(f32[2,512,128]{2,1,0:T(8,128)} %param.8) | copy-start | bytes 1572868
  12.5 7.4 %copy-start.2 = (f32[2,512,128]{2,1,0:T(8,128)S(1)}, f32[2,512,128]{2,1,0:T(8,128)}, u32[]{:S(2)}) copy-start(f32[2,512,128]{2,1,0:T(8,128)} %param.7) | copy-start | bytes 1572868
  12.5 7.4 %copy-start.3 = (s32[2,512,128]{2,1,0:T(8,128)S(1)}, s32[2,512,128]{2,1,0:T(8,128)}, u32[]{:S(2)}) copy-start(s32[2,512,128]{2,1,0:T(8,128)} %param.9) | copy-start | bytes 1572868
  12.5 7.4 %copy-start.8 = (f32[2,512,128]{2,1,0:T(8,128)S(1)}, f32[2,512,128]{2,1,0:T(8,128)}, u32[]{:S(2)}) copy-start(f32[2,512,128]{2,1,0:T(8,128)} %param.11) | copy-start | bytes 1572868
  13.4 6.5 %copy-start = (s32[2,512,128]{2,1,0:T(8,128)S(1)}, s32[2,512,128]{2,1,0:T(8,128)}, u32[]{:S(2)}) copy-start(s32[2,512,128]{2,1,0:T(8,128)} %param.10) | copy-start | bytes 1572868
  13.5 2.7 %collective-permute-start.2 = (f32[2,512,25]{1,2,0:T(8,128)S(1)}, f32[2,512,25]{1,2,0:T(8,128)S(1)}, u32[]{:S(2)}, u32[]{:S(2)}) collective-permute-start(f32[2,512,25]{1,2,0:T(8,128)S(1)} %get-tuple-element.54), channel_id=1, source_target_pairs={{0,1},{1,2},{2,3},{4,5},{5,6},{6,7},{8,9},{9,10},{10,11},{12,13},{... | collective-permute-start | bytes 307208 | tf_op jit(solution)/shard_map/ppermute | solution.py:24
  14.9 5.0 %collective-permute-start.3 = (f32[2,512,25]{1,2,0:T(8,128)S(1)}, f32[2,512,25]{1,2,0:T(8,128)S(1)}, u32[]{:S(2)}, u32[]{:S(2)}) collective-permute-start(f32[2,512,25]{1,2,0:T(8,128)S(1)} %get-tuple-element.55), channel_id=1, source_target_pairs={{1,0},{2,1},{3,2},{5,4},{6,5},{7,6},{9,8},{10,9},{11,10},{13,12},{... | collective-permute-start | bytes 307208 | tf_op jit(solution)/shard_map/ppermute | solution.py:26
  22.5 6.1 %collective-permute-start.5 = (f32[2,25,128]{2,1,0:T(8,128)S(1)}, f32[2,25,128]{2,1,0:T(8,128)S(1)}, u32[]{:S(2)}, u32[]{:S(2)}) collective-permute-start(f32[2,25,128]{2,1,0:T(8,128)S(1)} %get-tuple-element.50), channel_id=1, source_target_pairs={{0,4},{1,5},{2,6},{3,7},{8,12},{9,13},{10,14},{11,15},{16,20},{17,... | collective-permute-start | bytes 76808 | tf_op jit(solution)/shard_map/ppermute | solution.py:24
  27.0 5.8 %collective-permute-start.6 = (f32[2,25,128]{2,1,0:T(8,128)S(1)}, f32[2,25,128]{2,1,0:T(8,128)S(1)}, u32[]{:S(2)}, u32[]{:S(2)}) collective-permute-start(f32[2,25,128]{2,1,0:T(8,128)S(1)} %get-tuple-element.51), channel_id=1, source_target_pairs={{4,0},{5,1},{6,2},{7,3},{12,8},{13,9},{14,10},{15,11},{20,16},{21,... | collective-permute-start | bytes 76808 | tf_op jit(solution)/shard_map/ppermute | solution.py:26
  33.8 6.7 %collective-permute-start.7 = (f32[2,512,25]{1,2,0:T(8,128)S(1)}, f32[2,512,25]{1,2,0:T(8,128)S(1)}, u32[]{:S(2)}, u32[]{:S(2)}) collective-permute-start(f32[2,512,25]{1,2,0:T(8,128)S(1)} %get-tuple-element.48), channel_id=1, source_target_pairs={{0,1},{1,2},{2,3},{4,5},{5,6},{6,7},{8,9},{9,10},{10,11},{12,13},{... | collective-permute-start | bytes 307208 | tf_op jit(solution)/shard_map/ppermute | solution.py:24
  37.8 4.0 %collective-permute-start.8 = (f32[2,512,25]{1,2,0:T(8,128)S(1)}, f32[2,512,25]{1,2,0:T(8,128)S(1)}, u32[]{:S(2)}, u32[]{:S(2)}) collective-permute-start(f32[2,512,25]{1,2,0:T(8,128)S(1)} %get-tuple-element.49), channel_id=1, source_target_pairs={{1,0},{2,1},{3,2},{5,4},{6,5},{7,6},{9,8},{10,9},{11,10},{13,12},{... | collective-permute-start | bytes 307208 | tf_op jit(solution)/shard_map/ppermute | solution.py:26
  39.2 12.8 %collective-permute-start.9 = (f32[1,512,128]{2,1,0:T(8,128)S(1)}, f32[1,512,128]{2,1,0:T(8,128)S(1)}, u32[]{:S(2)}, u32[]{:S(2)}) collective-permute-start(f32[1,512,128]{2,1,0:T(8,128)S(1)} %get-tuple-element.43), channel_id=1, source_target_pairs={{8,0},{16,8},{24,16},{9,1},{17,9},{25,17},{10,2},{18,10},{26,18},{... | collective-permute-start | bytes 786440 | tf_op jit(solution)/shard_map/ppermute | solution.py:36
  43.6 8.4 %copy-start.14 = (f32[2,512,128]{2,1,0:T(8,128)}, f32[2,512,128]{2,1,0:T(8,128)S(1)}, u32[]{:S(2)}) copy-start(f32[2,512,128]{2,1,0:T(8,128)S(1)} %get-tuple-element.60) | copy-start | bytes 1572868
  43.6 3.2 %collective-permute-start.10 = (f32[2,25,128]{2,1,0:T(8,128)S(1)}, f32[2,25,128]{2,1,0:T(8,128)S(1)}, u32[]{:S(2)}, u32[]{:S(2)}) collective-permute-start(f32[2,25,128]{2,1,0:T(8,128)S(1)} %get-tuple-element.46), channel_id=1, source_target_pairs={{0,4},{1,5},{2,6},{3,7},{8,12},{9,13},{10,14},{11,15},{16,20},{17,... | collective-permute-start | bytes 76808 | tf_op jit(solution)/shard_map/ppermute | solution.py:24
  45.2 5.8 %collective-permute-start.11 = (f32[2,25,128]{2,1,0:T(8,128)S(1)}, f32[2,25,128]{2,1,0:T(8,128)S(1)}, u32[]{:S(2)}, u32[]{:S(2)}) collective-permute-start(f32[2,25,128]{2,1,0:T(8,128)S(1)} %get-tuple-element.47), channel_id=1, source_target_pairs={{4,0},{5,1},{6,2},{7,3},{12,8},{13,9},{14,10},{15,11},{20,16},{21,... | collective-permute-start | bytes 76808 | tf_op jit(solution)/shard_map/ppermute | solution.py:26
  46.6 5.4 %copy-start.5 = (f32[2,512,128]{2,1,0:T(8,128)S(1)}, f32[2,512,128]{2,1,0:T(8,128)}, u32[]{:S(2)}) copy-start(f32[2,512,128]{2,1,0:T(8,128)} %param.13) | copy-start | bytes 1572868
  52.0 4.5 %copy-start.7 = (f32[2,512,128]{1,2,0:T(8,128)}, f32[2,512,128]{1,2,0:T(8,128)S(1)}, u32[]{:S(2)}) copy-start(f32[2,512,128]{1,2,0:T(8,128)S(1)} %convolution_bitcast_fusion.3) | copy-start | bytes 1572868
  52.9 53.5 %collective-permute-start.14 = (f32[1,512,128]{2,1,0:T(8,128)S(1)}, f32[1,512,128]{2,1,0:T(8,128)S(1)}, u32[]{:S(2)}, u32[]{:S(2)}) collective-permute-start(f32[1,512,128]{2,1,0:T(8,128)S(1)} %get-tuple-element.40), channel_id=1, source_target_pairs={{0,8},{8,16},{16,24},{1,9},{9,17},{17,25},{2,10},{10,18},{18,26},{... | collective-permute-start | bytes 786440 | tf_op jit(solution)/shard_map/ppermute | solution.py:36
  57.2 49.2 %collective-permute-start.12 = (f32[2,512,25]{1,2,0:T(8,128)}, f32[2,512,25]{1,2,0:T(8,128)}, u32[]{:S(2)}, u32[]{:S(2)}) collective-permute-start(f32[2,512,25]{1,2,0:T(8,128)} %get-tuple-element.44), channel_id=1, source_target_pairs={{0,1},{1,2},{2,3},{4,5},{5,6},{6,7},{8,9},{9,10},{10,11},{12,13},{... | collective-permute-start | bytes 307208 | tf_op jit(solution)/shard_map/ppermute | solution.py:24
  61.9 44.6 %collective-permute-start.13 = (f32[2,512,25]{1,2,0:T(8,128)}, f32[2,512,25]{1,2,0:T(8,128)}, u32[]{:S(2)}, u32[]{:S(2)}) collective-permute-start(f32[2,512,25]{1,2,0:T(8,128)} %get-tuple-element.45), channel_id=1, source_target_pairs={{1,0},{2,1},{3,2},{5,4},{6,5},{7,6},{9,8},{10,9},{11,10},{13,12},{... | collective-permute-start | bytes 307208 | tf_op jit(solution)/shard_map/ppermute | solution.py:26
  106.5 0.7 copy-start.10
  111.1 5.8 %collective-permute-start.15 = (f32[2,25,128]{2,1,0:T(8,128)S(1)}, f32[2,25,128]{2,1,0:T(8,128)S(1)}, u32[]{:S(2)}, u32[]{:S(2)}) collective-permute-start(f32[2,25,128]{2,1,0:T(8,128)S(1)} %get-tuple-element.38), channel_id=1, source_target_pairs={{0,4},{1,5},{2,6},{3,7},{8,12},{9,13},{10,14},{11,15},{16,20},{17,... | collective-permute-start | bytes 76808 | tf_op jit(solution)/shard_map/ppermute | solution.py:24
  115.2 5.8 %collective-permute-start.16 = (f32[2,25,128]{2,1,0:T(8,128)S(1)}, f32[2,25,128]{2,1,0:T(8,128)S(1)}, u32[]{:S(2)}, u32[]{:S(2)}) collective-permute-start(f32[2,25,128]{2,1,0:T(8,128)S(1)} %get-tuple-element.39), channel_id=1, source_target_pairs={{4,0},{5,1},{6,2},{7,3},{12,8},{13,9},{14,10},{15,11},{20,16},{21,... | collective-permute-start | bytes 76808 | tf_op jit(solution)/shard_map/ppermute | solution.py:26
  122.0 4.1 %collective-permute-start.17 = (f32[2,512,25]{1,2,0:T(8,128)S(1)}, f32[2,512,25]{1,2,0:T(8,128)S(1)}, u32[]{:S(2)}, u32[]{:S(2)}) collective-permute-start(f32[2,512,25]{1,2,0:T(8,128)S(1)} %get-tuple-element.36), channel_id=1, source_target_pairs={{0,1},{1,2},{2,3},{4,5},{5,6},{6,7},{8,9},{9,10},{10,11},{12,13},{... | collective-permute-start | bytes 307208 | tf_op jit(solution)/shard_map/ppermute | solution.py:24
  123.3 5.8 %copy-start.15 = (f32[2,512,128]{2,1,0:T(8,128)S(1)}, f32[2,512,128]{2,1,0:T(8,128)}, u32[]{:S(2)}) copy-start(f32[2,512,128]{2,1,0:T(8,128)} %copy-done.14) | copy-start | bytes 1572868
  123.3 5.7 %collective-permute-start.18 = (f32[2,512,25]{1,2,0:T(8,128)S(1)}, f32[2,512,25]{1,2,0:T(8,128)S(1)}, u32[]{:S(2)}, u32[]{:S(2)}) collective-permute-start(f32[2,512,25]{1,2,0:T(8,128)S(1)} %get-tuple-element.37), channel_id=1, source_target_pairs={{1,0},{2,1},{3,2},{5,4},{6,5},{7,6},{9,8},{10,9},{11,10},{13,12},{... | collective-permute-start | bytes 307208 | tf_op jit(solution)/shard_map/ppermute | solution.py:26
  124.8 14.4 %collective-permute-start.19 = (f32[1,512,128]{2,1,0:T(8,128)S(1)}, f32[1,512,128]{2,1,0:T(8,128)S(1)}, u32[]{:S(2)}, u32[]{:S(2)}) collective-permute-start(f32[1,512,128]{2,1,0:T(8,128)S(1)} %get-tuple-element.31), channel_id=1, source_target_pairs={{8,0},{16,8},{24,16},{9,1},{17,9},{25,17},{10,2},{18,10},{26,18},{... | collective-permute-start | bytes 786440 | tf_op jit(solution)/shard_map/ppermute | solution.py:36
  130.8 8.4 %copy-start.12 = (f32[2,512,128]{2,1,0:T(8,128)}, f32[2,512,128]{2,1,0:T(8,128)S(1)}, u32[]{:S(2)}) copy-start(f32[2,512,128]{2,1,0:T(8,128)S(1)} %get-tuple-element.63) | copy-start | bytes 1572868
  130.8 3.2 %collective-permute-start.20 = (f32[2,25,128]{2,1,0:T(8,128)S(1)}, f32[2,25,128]{2,1,0:T(8,128)S(1)}, u32[]{:S(2)}, u32[]{:S(2)}) collective-permute-start(f32[2,25,128]{2,1,0:T(8,128)S(1)} %get-tuple-element.34), channel_id=1, source_target_pairs={{0,4},{1,5},{2,6},{3,7},{8,12},{9,13},{10,14},{11,15},{16,20},{17,... | collective-permute-start | bytes 76808 | tf_op jit(solution)/shard_map/ppermute | solution.py:24
  132.4 5.8 %collective-permute-start.21 = (f32[2,25,128]{2,1,0:T(8,128)S(1)}, f32[2,25,128]{2,1,0:T(8,128)S(1)}, u32[]{:S(2)}, u32[]{:S(2)}) collective-permute-start(f32[2,25,128]{2,1,0:T(8,128)S(1)} %get-tuple-element.35), channel_id=1, source_target_pairs={{4,0},{5,1},{6,2},{7,3},{12,8},{13,9},{14,10},{15,11},{20,16},{21,... | collective-permute-start | bytes 76808 | tf_op jit(solution)/shard_map/ppermute | solution.py:26
  139.1 3.4 %copy-start.6 = (f32[2,512,128]{1,2,0:T(8,128)}, f32[2,512,128]{1,2,0:T(8,128)S(1)}, u32[]{:S(2)}) copy-start(f32[2,512,128]{1,2,0:T(8,128)S(1)} %convolution_bitcast_fusion.1) | copy-start | bytes 1572868
  140.2 53.2 %copy-start.4 = (s32[2,512,128]{2,1,0:T(8,128)S(1)}, s32[2,512,128]{2,1,0:T(8,128)}, u32[]{:S(2)}) copy-start(s32[2,512,128]{2,1,0:T(8,128)} %param.9) | copy-start | bytes 1572868
  140.2 52.5 %collective-permute-start.24 = (f32[1,512,128]{2,1,0:T(8,128)S(1)}, f32[1,512,128]{2,1,0:T(8,128)S(1)}, u32[]{:S(2)}, u32[]{:S(2)}) collective-permute-start(f32[1,512,128]{2,1,0:T(8,128)S(1)} %get-tuple-element.28), channel_id=1, source_target_pairs={{0,8},{8,16},{16,24},{1,9},{9,17},{17,25},{2,10},{10,18},{18,26},{... | collective-permute-start | bytes 786440 | tf_op jit(solution)/shard_map/ppermute | solution.py:36
  143.3 49.4 %collective-permute-start.22 = (f32[2,512,25]{1,2,0:T(8,128)}, f32[2,512,25]{1,2,0:T(8,128)}, u32[]{:S(2)}, u32[]{:S(2)}) collective-permute-start(f32[2,512,25]{1,2,0:T(8,128)} %get-tuple-element.32), channel_id=1, source_target_pairs={{0,1},{1,2},{2,3},{4,5},{5,6},{6,7},{8,9},{9,10},{10,11},{12,13},{... | collective-permute-start | bytes 307208 | tf_op jit(solution)/shard_map/ppermute | solution.py:24
  148.0 44.7 %collective-permute-start.23 = (f32[2,512,25]{1,2,0:T(8,128)}, f32[2,512,25]{1,2,0:T(8,128)}, u32[]{:S(2)}, u32[]{:S(2)}) collective-permute-start(f32[2,512,25]{1,2,0:T(8,128)} %get-tuple-element.33), channel_id=1, source_target_pairs={{1,0},{2,1},{3,2},{5,4},{6,5},{7,6},{9,8},{10,9},{11,10},{13,12},{... | collective-permute-start | bytes 307208 | tf_op jit(solution)/shard_map/ppermute | solution.py:26
  192.7 0.7 copy-start.9
  197.3 5.8 %collective-permute-start.25 = (f32[2,25,128]{2,1,0:T(8,128)S(1)}, f32[2,25,128]{2,1,0:T(8,128)S(1)}, u32[]{:S(2)}, u32[]{:S(2)}) collective-permute-start(f32[2,25,128]{2,1,0:T(8,128)S(1)} %get-tuple-element.26), channel_id=1, source_target_pairs={{0,4},{1,5},{2,6},{3,7},{8,12},{9,13},{10,14},{11,15},{16,20},{17,... | collective-permute-start | bytes 76808 | tf_op jit(solution)/shard_map/ppermute | solution.py:24
  201.5 5.8 %collective-permute-start.26 = (f32[2,25,128]{2,1,0:T(8,128)S(1)}, f32[2,25,128]{2,1,0:T(8,128)S(1)}, u32[]{:S(2)}, u32[]{:S(2)}) collective-permute-start(f32[2,25,128]{2,1,0:T(8,128)S(1)} %get-tuple-element.27), channel_id=1, source_target_pairs={{4,0},{5,1},{6,2},{7,3},{12,8},{13,9},{14,10},{15,11},{20,16},{21,... | collective-permute-start | bytes 76808 | tf_op jit(solution)/shard_map/ppermute | solution.py:26
  208.2 4.1 %collective-permute-start.27 = (f32[2,512,25]{1,2,0:T(8,128)S(1)}, f32[2,512,25]{1,2,0:T(8,128)S(1)}, u32[]{:S(2)}, u32[]{:S(2)}) collective-permute-start(f32[2,512,25]{1,2,0:T(8,128)S(1)} %get-tuple-element.24), channel_id=1, source_target_pairs={{0,1},{1,2},{2,3},{4,5},{5,6},{6,7},{8,9},{9,10},{10,11},{12,13},{... | collective-permute-start | bytes 307208 | tf_op jit(solution)/shard_map/ppermute | solution.py:24
  209.5 5.7 %copy-start.13 = (f32[2,512,128]{2,1,0:T(8,128)S(1)}, f32[2,512,128]{2,1,0:T(8,128)}, u32[]{:S(2)}) copy-start(f32[2,512,128]{2,1,0:T(8,128)} %copy-done.12) | copy-start | bytes 1572868
  209.5 5.7 %collective-permute-start.28 = (f32[2,512,25]{1,2,0:T(8,128)S(1)}, f32[2,512,25]{1,2,0:T(8,128)S(1)}, u32[]{:S(2)}, u32[]{:S(2)}) collective-permute-start(f32[2,512,25]{1,2,0:T(8,128)S(1)} %get-tuple-element.25), channel_id=1, source_target_pairs={{1,0},{2,1},{3,2},{5,4},{6,5},{7,6},{9,8},{10,9},{11,10},{13,12},{... | collective-permute-start | bytes 307208 | tf_op jit(solution)/shard_map/ppermute | solution.py:26
  211.0 8.6 %collective-permute-start.29 = (f32[1,512,128]{2,1,0:T(8,128)S(1)}, f32[1,512,128]{2,1,0:T(8,128)S(1)}, u32[]{:S(2)}, u32[]{:S(2)}) collective-permute-start(f32[1,512,128]{2,1,0:T(8,128)S(1)} %get-tuple-element.23), channel_id=1, source_target_pairs={{8,0},{16,8},{24,16},{9,1},{17,9},{25,17},{10,2},{18,10},{26,18},{... | collective-permute-start | bytes 786440 | tf_op jit(solution)/shard_map/ppermute | solution.py:36
where the time goes:
time: 269 us; the launch traced here: 268 us
  blocking collectives  124 us (46%)
  starting transfers between devices  67.7 us (25%)
  waiting for transfers between devices  35 us (13%)
  matrix products  21.7 us (8%)
  between operations  10.6 us (4%)
  other arithmetic  4.76 us (2%)
  local copies, waits for them, and re-layouts  4.08 us (2%)
    psum x3, blocking collectives, local(): lax.psum((primal_sum, dual_sum), ('layer', 'row', 'col'))  124 us
    ppermute x12, starting transfers between devices, extended(): lax.ppermute(tail, axis, [(i, (i + 1) % count) for i in range(ends)])  38.4 us
    ppermute x12, waiting for transfers between devices, extended(): lax.ppermute(head, axis, [((i + 1) % count, i) for i in range(ends)])  32.1 us
    dot_general x6, matrix products, cols_pass(): jnp.einsum('liq,qj->lij', partial_sum, col_band, precision=lax.Precision....  16.3 us
    ppermute x12, starting transfers between devices, extended(): lax.ppermute(head, axis, [((i + 1) % count, i) for i in range(ends)])  15.9 us
    ppermute x6, starting transfers between devices, from_behind(): return lax.ppermute(block, axis, route)  13.4 us
    dot_general x6, matrix products, rows_pass(): jnp.einsum('ip,lpq->liq', row_band, padded, precision=lax.Precision.HIGHEST)  5.39 us
  transfers between devices with their start and end apart: 30, of which 15 were waited for; matrix products, arithmetic and copies ran while one was open for 4% of the time, Pallas kernels for 0%

commit v1 on v0

--- a/solution.py
+++ b/solution.py
@@ -110,7 +110,15 @@
         density_move = density_new - density_dual
         stacked_move = stacked_new - stacked_dual
         dual_sum = jnp.sum(density_move * density_move) + jnp.sum(stacked_move * stacked_move)
-        primal_sum, dual_sum = lax.psum((primal_sum, dual_sum), ("layer", "row", "col"))
+
+        def connect_record(unit):
+            device_axis = "layer"
+            axis_tag = ("row", "col")
+            for dev_j in (axis_tag, device_axis):
+                unit = lax.psum(unit, axis_name=dev_j)
+            return unit
+
+        primal_sum, dual_sum = connect_record((primal_sum, dual_sum))
         weight = jnp.sqrt(weight) * jnp.sqrt(
             jnp.sqrt((dual_sum + tiny_term) / (primal_sum + tiny_term))
         )

time: 269 us -> 215 us (0.80)
  blocking collectives: 124 us -> 71.2 us
    psum x3 -> x6, blocking collectives: 124 us -> 71.2 us  [connect_record(): unit = lax.psum(unit, axis_name=dev_j)]
    ppermute x6, waiting for transfers between devices: 1.77 us -> 6.5 us  [from_behind(): return lax.ppermute(block, axis, route)]
    ppermute x12, waiting for transfers between devices: 32.1 us -> 27.3 us  [extended(): lax.ppermute(head, axis, [((i + 1) % count, i) for i in range(ends)])]
    ppermute x12, starting transfers between devices: 38.4 us -> 35.6 us  [extended(): lax.ppermute(tail, axis, [(i, (i + 1) % count) for i in range(ends)])]
  transfers between devices with their start and end apart: 30 -> 30, of which waited for: 15 -> 15; matrix products, arithmetic and copies ran while one was open for 4% -> 5% of each run, Pallas kernels for 0% -> 0%
where the time goes in v1:
time: 215 us; the launch traced here: 214 us
  blocking collectives  71.2 us (33%)
  starting transfers between devices  66.9 us (31%)
  waiting for transfers between devices  35 us (16%)
  matrix products  21.7 us (10%)
  between operations  10.2 us (5%)
  other arithmetic  4.7 us (2%)
  local copies, waits for them, and re-layouts  4.03 us (2%)
    psum x6, blocking collectives, connect_record(): unit = lax.psum(unit, axis_name=dev_j)  71.2 us
    ppermute x12, starting transfers between devices, extended(): lax.ppermute(tail, axis, [(i, (i + 1) % count) for i in range(ends)])  35.6 us
    ppermute x12, waiting for transfers between devices, extended(): lax.ppermute(head, axis, [((i + 1) % count, i) for i in range(ends)])  27.3 us
    dot_general x6, matrix products, cols_pass(): jnp.einsum('liq,qj->lij', partial_sum, col_band, precision=lax.Precision....  16.3 us
    ppermute x12, starting transfers between devices, extended(): lax.ppermute(head, axis, [((i + 1) % count, i) for i in range(ends)])  15.9 us
    ppermute x6, starting transfers between devices, from_behind(): return lax.ppermute(block, axis, route)  15.4 us
    ppermute x6, waiting for transfers between devices, from_behind(): return lax.ppermute(block, axis, route)  6.5 us
    dot_general x6, matrix products, rows_pass(): jnp.einsum('ip,lpq->liq', row_band, padded, precision=lax.Precision.HIGHEST)  5.39 us
  transfers between devices with their start and end apart: 30, of which 15 were waited for; matrix products, arithmetic and copies ran while one was open for 5% of the time, Pallas kernels for 0%

profile of v1, /device:TPU:0, one launch (start us, length us, event | category | flops | bytes accessed | tf_op | source)
XLA Modules:
  0.0 213.8 jit_solution(9699976677255762976)
XLA Ops:
  1.4 4.9 %collective-permute-start = (f32[2,25,128]{2,1,0:T(8,128)S(1)}, f32[2,25,128]{2,1,0:T(8,128)S(1)}, u32[]{:S(2)}, u32[]{:S(2)}) collective-permute-start(f32[2,25,128]{2,1,0:T(8,128)S(1)} %get-tuple-element.62), channel_id=1, source_target_pairs={{0,4},{1,5},{2,6},{3,7},{8,12},{9,13},{10,14},{11,15},{16,20},{17,... | collective-permute-start | bytes 76808 | tf_op jit(solution)/shard_map/ppermute | solution.py:24
  6.3 1.3 collective-permute-start.1
  8.8 3.6 %collective-permute-start.4 = (f32[1,512,128]{2,1,0:T(8,128)S(1)}, f32[1,512,128]{2,1,0:T(8,128)S(1)}, u32[]{:S(2)}, u32[]{:S(2)}) collective-permute-start(f32[1,512,128]{2,1,0:T(8,128)S(1)} %get-tuple-element.58), channel_id=1, source_target_pairs={{0,8},{8,16},{16,24},{1,9},{9,17},{17,25},{2,10},{10,18},{18,26},{... | collective-permute-start | bytes 786440 | tf_op jit(solution)/shard_map/ppermute | solution.py:36
  13.5 1.4 collective-permute-start.2
  14.9 1.3 collective-permute-start.3
  16.2 3.7 %collective-permute-done.3 = f32[2,512,25]{1,2,0:T(8,128)S(1)} collective-permute-done((f32[2,512,25]{1,2,0:T(8,128)S(1)}, f32[2,512,25]{1,2,0:T(8,128)S(1)}, u32[]{:S(2)}, u32[]{:S(2)}) %collective-permute-start.3) | collective-permute-done | bytes 102432 | tf_op jit(solution)/shard_map/ppermute | solution.py:26
  20.0 2.5 %multiply_reduce_fusion.6 = (f32[]{:T(128)}, f32[2,512,128]{2,1,0:T(8,128)S(1)}, f32[2,512,128]{2,1,0:T(8,128)}) fusion(f32[2,512,128]{2,1,0:T(8,128)S(1)} %copy-done.8, f32[2,512,128]{2,1,0:T(8,128)S(1)} %copy-done.1, f32[2,512,128]{2,1,0:T(8,128)S(1)} %broadcast_multiply_fusion, f32[1,512,128]{2,1,0:T(8,128)S(1)} %get-tuple-element.59, ...), kind=kOutput, calls=%fused_computation.144 | convolution fusion | flops 282915840 | bytes 5447684 | tf_op jit(solution)/shard_map/liq,qj->lij/dot_general | solution.py:51
  22.5 4.5 %collective-permute-start.5 = (f32[2,25,128]{2,1,0:T(8,128)S(1)}, f32[2,25,128]{2,1,0:T(8,128)S(1)}, u32[]{:S(2)}, u32[]{:S(2)}) collective-permute-start(f32[2,25,128]{2,1,0:T(8,128)S(1)} %get-tuple-element.56), channel_id=1, source_target_pairs={{0,4},{1,5},{2,6},{3,7},{8,12},{9,13},{10,14},{11,15},{16,20},{17,... | collective-permute-start | bytes 76808 | tf_op jit(solution)/shard_map/ppermute | solution.py:24
  27.0 1.3 collective-permute-start.6
  28.6 4.2 %collective-permute-done.6 = f32[2,25,128]{2,1,0:T(8,128)S(1)} collective-permute-done((f32[2,25,128]{2,1,0:T(8,128)S(1)}, f32[2,25,128]{2,1,0:T(8,128)S(1)}, u32[]{:S(2)}, u32[]{:S(2)}) %collective-permute-start.6) | collective-permute-done | bytes 25632 | tf_op jit(solution)/shard_map/ppermute | solution.py:26
  33.8 4.0 %collective-permute-start.7 = (f32[2,512,25]{1,2,0:T(8,128)S(1)}, f32[2,512,25]{1,2,0:T(8,128)S(1)}, u32[]{:S(2)}, u32[]{:S(2)}) collective-permute-start(f32[2,512,25]{1,2,0:T(8,128)S(1)} %get-tuple-element.54), channel_id=1, source_target_pairs={{0,1},{1,2},{2,3},{4,5},{5,6},{6,7},{8,9},{9,10},{10,11},{12,13},{... | collective-permute-start | bytes 307208 | tf_op jit(solution)/shard_map/ppermute | solution.py:24
  37.8 1.3 collective-permute-start.8
  39.2 1.3 collective-permute-start.9
  40.5 1.4 collective-permute-done.8
  41.9 1.7 multiply_reduce_fusion.8
  43.6 1.6 collective-permute-start.10
  45.2 1.3 collective-permute-start.11
  46.8 4.2 %collective-permute-done.11 = f32[2,25,128]{2,1,0:T(8,128)S(1)} collective-permute-done((f32[2,25,128]{2,1,0:T(8,128)S(1)}, f32[2,25,128]{2,1,0:T(8,128)S(1)}, u32[]{:S(2)}, u32[]{:S(2)}) %collective-permute-start.11) | collective-permute-done | bytes 25632 | tf_op jit(solution)/shard_map/ppermute | solution.py:26
  52.9 3.5 %collective-permute-start.14 = (f32[1,512,128]{2,1,0:T(8,128)S(1)}, f32[1,512,128]{2,1,0:T(8,128)S(1)}, u32[]{:S(2)}, u32[]{:S(2)}) collective-permute-start(f32[1,512,128]{2,1,0:T(8,128)S(1)} %get-tuple-element.46), channel_id=1, source_target_pairs={{0,8},{8,16},{16,24},{1,9},{9,17},{17,25},{2,10},{10,18},{18,26},{... | collective-permute-start | bytes 786440 | tf_op jit(solution)/shard_map/ppermute | solution.py:36
  57.1 4.7 %collective-permute-start.12 = (f32[2,512,25]{1,2,0:T(8,128)}, f32[2,512,25]{1,2,0:T(8,128)}, u32[]{:S(2)}, u32[]{:S(2)}) collective-permute-start(f32[2,512,25]{1,2,0:T(8,128)} %get-tuple-element.50), channel_id=1, source_target_pairs={{0,1},{1,2},{2,3},{4,5},{5,6},{6,7},{8,9},{9,10},{10,11},{12,13},{... | collective-permute-start | bytes 307208 | tf_op jit(solution)/shard_map/ppermute | solution.py:24
  64.3 13.8 %all-reduce.2 = (f32[]{:T(128)}, f32[]{:T(128)}) all-reduce(f32[]{:T(128)S(6)} %add.127, f32[]{:T(128)} %get-tuple-element.26), channel_id=1, replica_groups=mesh['layer'=4,'row'=2,'col'=4] {'row','col'}, use_global_device_ids=true, to_apply=%region_2.3 | all-reduce | flops 2 | bytes 16 | tf_op jit(solution)/shard_map/psum | solution.py:118
  78.1 10.5 %all-reduce.5 = (f32[]{:T(128)}, f32[]{:T(128)}) all-reduce(f32[]{:T(128)} %get-tuple-element.8, f32[]{:T(128)} %get-tuple-element.9), channel_id=1, replica_groups=mesh['layer'=4,'row'=2,'col'=4] {'layer'}, use_global_device_ids=true, to_apply=%region_3.4 | all-reduce | flops 2 | bytes 16 | tf_op jit(solution)/shard_map/psum | solution.py:118
  90.7 3.9 %multiply_reduce_fusion.3 = (f32[]{:T(128)}, f32[2,512,128]{2,1,0:T(8,128)S(1)}, f32[2,512,128]{2,1,0:T(8,128)}) fusion(f32[2,512,128]{2,1,0:T(8,128)} %get-tuple-element.64, f32[2,512,128]{2,1,0:T(8,128)S(1)} %copy-done.1, f32[2,512,128]{2,1,0:T(8,128)S(1)} %get-tuple-element.21, f32[1,512,128]{2,1,0:T(8,128)S(1)} %get-tuple-element.47, ...), kind=kOutput, calls=%fused_computation.139 | convolution fusion | flops 282915840 | bytes 5447688 | tf_op jit(solution)/shard_map/liq,qj->lij/dot_general | solution.py:51
  94.6 4.0 %collective-permute-start.15 = (f32[2,25,128]{2,1,0:T(8,128)S(1)}, f32[2,25,128]{2,1,0:T(8,128)S(1)}, u32[]{:S(2)}, u32[]{:S(2)}) collective-permute-start(f32[2,25,128]{2,1,0:T(8,128)S(1)} %get-tuple-element.44), channel_id=1, source_target_pairs={{0,4},{1,5},{2,6},{3,7},{8,12},{9,13},{10,14},{11,15},{16,20},{17,... | collective-permute-start | bytes 76808 | tf_op jit(solution)/shard_map/ppermute | solution.py:24
  98.6 1.3 collective-permute-start.16
  100.2 4.2 %collective-permute-done.16 = f32[2,25,128]{2,1,0:T(8,128)S(1)} collective-permute-done((f32[2,25,128]{2,1,0:T(8,128)S(1)}, f32[2,25,128]{2,1,0:T(8,128)S(1)}, u32[]{:S(2)}, u32[]{:S(2)}) %collective-permute-start.16) | collective-permute-done | bytes 25632 | tf_op jit(solution)/shard_map/ppermute | solution.py:26
  105.4 1.3 collective-permute-start.17
  106.7 1.4 collective-permute-start.18
  108.2 1.3 collective-permute-start.19
  110.1 1.7 multiply_reduce_fusion.5
  111.8 1.6 collective-permute-start.20
  113.4 1.5 collective-permute-start.21
  115.0 4.2 %collective-permute-done.21 = f32[2,25,128]{2,1,0:T(8,128)S(1)} collective-permute-done((f32[2,25,128]{2,1,0:T(8,128)S(1)}, f32[2,25,128]{2,1,0:T(8,128)S(1)}, u32[]{:S(2)}, u32[]{:S(2)}) %collective-permute-start.21) | collective-permute-done | bytes 25632 | tf_op jit(solution)/shard_map/ppermute | solution.py:26
  121.1 4.4 %collective-permute-start.24 = (f32[1,512,128]{2,1,0:T(8,128)S(1)}, f32[1,512,128]{2,1,0:T(8,128)S(1)}, u32[]{:S(2)}, u32[]{:S(2)}) collective-permute-start(f32[1,512,128]{2,1,0:T(8,128)S(1)} %get-tuple-element.34), channel_id=1, source_target_pairs={{0,8},{8,16},{16,24},{1,9},{9,17},{17,25},{2,10},{10,18},{18,26},{... | collective-permute-start | bytes 786440 | tf_op jit(solution)/shard_map/ppermute | solution.py:36
  126.2 2.3 %collective-permute-start.22 = (f32[2,512,25]{1,2,0:T(8,128)}, f32[2,512,25]{1,2,0:T(8,128)}, u32[]{:S(2)}, u32[]{:S(2)}) collective-permute-start(f32[2,512,25]{1,2,0:T(8,128)} %get-tuple-element.38), channel_id=1, source_target_pairs={{0,1},{1,2},{2,3},{4,5},{5,6},{6,7},{8,9},{9,10},{10,11},{12,13},{... | collective-permute-start | bytes 307208 | tf_op jit(solution)/shard_map/ppermute | solution.py:24
  131.0 14.5 %all-reduce.1 = (f32[]{:T(128)}, f32[]{:T(128)}) all-reduce(f32[]{:T(128)S(6)} %add.136, f32[]{:T(128)} %get-tuple-element.24), channel_id=1, replica_groups=mesh['layer'=4,'row'=2,'col'=4] {'row','col'}, use_global_device_ids=true, to_apply=%region_9.10 | all-reduce | flops 2 | bytes 16 | tf_op jit(solution)/shard_map/psum | solution.py:118
  145.5 9.5 %all-reduce.4 = (f32[]{:T(128)}, f32[]{:T(128)}) all-reduce(f32[]{:T(128)} %get-tuple-element.6, f32[]{:T(128)} %get-tuple-element.7), channel_id=1, replica_groups=mesh['layer'=4,'row'=2,'col'=4] {'layer'}, use_global_device_ids=true, to_apply=%region_10.11 | all-reduce | flops 2 | bytes 16 | tf_op jit(solution)/shard_map/psum | solution.py:118
  157.2 3.9 %multiply_reduce_fusion = (f32[]{:T(128)}, f32[2,512,128]{2,1,0:T(8,128)S(1)}, f32[2,512,128]{2,1,0:T(8,128)}) fusion(f32[2,512,128]{2,1,0:T(8,128)} %get-tuple-element.67, f32[2,512,128]{2,1,0:T(8,128)S(1)} %copy-done.1, f32[2,512,128]{2,1,0:T(8,128)S(1)} %get-tuple-element.19, f32[1,512,128]{2,1,0:T(8,128)S(1)} %get-tuple-element.35, ...), kind=kOutput, calls=%fused_computation.134 | convolution fusion | flops 282915840 | bytes 5447688 | tf_op jit(solution)/shard_map/liq,qj->lij/dot_general | solution.py:51
  161.1 4.0 %collective-permute-start.25 = (f32[2,25,128]{2,1,0:T(8,128)S(1)}, f32[2,25,128]{2,1,0:T(8,128)S(1)}, u32[]{:S(2)}, u32[]{:S(2)}) collective-permute-start(f32[2,25,128]{2,1,0:T(8,128)S(1)} %get-tuple-element.32), channel_id=1, source_target_pairs={{0,4},{1,5},{2,6},{3,7},{8,12},{9,13},{10,14},{11,15},{16,20},{17,... | collective-permute-start | bytes 76808 | tf_op jit(solution)/shard_map/ppermute | solution.py:24
  165.1 1.3 collective-permute-start.26
  166.7 4.2 %collective-permute-done.26 = f32[2,25,128]{2,1,0:T(8,128)S(1)} collective-permute-done((f32[2,25,128]{2,1,0:T(8,128)S(1)}, f32[2,25,128]{2,1,0:T(8,128)S(1)}, u32[]{:S(2)}, u32[]{:S(2)}) %collective-permute-start.26) | collective-permute-done | bytes 25632 | tf_op jit(solution)/shard_map/ppermute | solution.py:26
  171.8 1.3 collective-permute-start.27
  173.1 1.4 collective-permute-start.28
  176.5 2.5 %multiply_reduce_fusion.2 = (f32[]{:T(128)}, f32[2,512,128]{2,1,0:T(8,128)}) fusion(f32[2,512,128]{2,1,0:T(8,128)S(1)} %copy-done.13, pred[2,512,128]{2,1,0:T(32,128)(4,1)S(1)} %broadcast_compare_fusion, f32[2,512,25]{1,2,0:T(8,128)S(1)} %collective-permute-done.28, f32[2,512,128]{1,2,0:T(8,128)S(1)} %convolution_bitcast_fusion, ...), kind=kOutput, calls=%fused_computation.136 | convolution fusion | flops 281867264 | bytes 1908744 | tf_op jit(solution)/shard_map/liq,qj->lij/dot_general | solution.py:51
  179.0 6.5 %collective-permute-done.29 = f32[1,512,128]{2,1,0:T(8,128)S(1)} collective-permute-done((f32[1,512,128]{2,1,0:T(8,128)S(1)}, f32[1,512,128]{2,1,0:T(8,128)S(1)}, u32[]{:S(2)}, u32[]{:S(2)}) %collective-permute-start.29) | collective-permute-done | bytes 262176 | tf_op jit(solution)/shard_map/ppermute | solution.py:36
  185.5 1.6 multiply_reduce_fusion.1
  188.3 12.6 %all-reduce = (f32[]{:T(128)}, f32[]{:T(128)}) all-reduce(f32[]{:T(128)S(6)} %add.145, f32[]{:T(128)} %get-tuple-element.22), channel_id=1, replica_groups=mesh['layer'=4,'row'=2,'col'=4] {'row','col'}, use_global_device_ids=true, to_apply=%region_16.17 | all-reduce | flops 2 | bytes 16 | tf_op jit(solution)/shard_map/psum | solution.py:118
  200.9 10.4 %all-reduce.3 = (f32[]{:T(128)}, f32[]{:T(128)}) all-reduce(f32[]{:T(128)} %get-tuple-element.4, f32[]{:T(128)} %get-tuple-element.5), channel_id=1, replica_groups=mesh['layer'=4,'row'=2,'col'=4] {'layer'}, use_global_device_ids=true, to_apply=%region_17.18 | all-reduce | flops 2 | bytes 16 | tf_op jit(solution)/shard_map/psum | solution.py:118
  (87 shorter events, 18.6 us)
Async XLA Ops:
  1.4 11.0 %collective-permute-start = (f32[2,25,128]{2,1,0:T(8,128)S(1)}, f32[2,25,128]{2,1,0:T(8,128)S(1)}, u32[]{:S(2)}, u32[]{:S(2)}) collective-permute-start(f32[2,25,128]{2,1,0:T(8,128)S(1)} %get-tuple-element.62), channel_id=1, source_target_pairs={{0,4},{1,5},{2,6},{3,7},{8,12},{9,13},{10,14},{11,15},{16,20},{17,... | collective-permute-start | bytes 76808 | tf_op jit(solution)/shard_map/ppermute | solution.py:24
  6.3 6.2 %collective-permute-start.1 = (f32[2,25,128]{2,1,0:T(8,128)S(1)}, f32[2,25,128]{2,1,0:T(8,128)S(1)}, u32[]{:S(2)}, u32[]{:S(2)}) collective-permute-start(f32[2,25,128]{2,1,0:T(8,128)S(1)} %get-tuple-element.63), channel_id=1, source_target_pairs={{4,0},{5,1},{6,2},{7,3},{12,8},{13,9},{14,10},{15,11},{20,16},{21,... | collective-permute-start | bytes 76808 | tf_op jit(solution)/shard_map/ppermute | solution.py:26
  8.8 3.7 %copy-start.11 = (f32[2,512,128]{2,1,0:T(8,128)S(1)}, f32[2,512,128]{2,1,0:T(8,128)}, u32[]{:S(2)}) copy-start(f32[2,512,128]{2,1,0:T(8,128)} %param.12) | copy-start | bytes 1572868
  8.8 11.1 %collective-permute-start.4 = (f32[1,512,128]{2,1,0:T(8,128)S(1)}, f32[1,512,128]{2,1,0:T(8,128)S(1)}, u32[]{:S(2)}, u32[]{:S(2)}) collective-permute-start(f32[1,512,128]{2,1,0:T(8,128)S(1)} %get-tuple-element.58), channel_id=1, source_target_pairs={{0,8},{8,16},{16,24},{1,9},{9,17},{17,25},{2,10},{10,18},{18,26},{... | collective-permute-start | bytes 786440 | tf_op jit(solution)/shard_map/ppermute | solution.py:36
  12.5 7.4 %copy-start.1 = (f32[2,512,128]{2,1,0:T(8,128)S(1)}, f32[2,512,128]{2,1,0:T(8,128)}, u32[]{:S(2)}) copy-start(f32[2,512,128]{2,1,0:T(8,128)} %param.8) | copy-start | bytes 1572868
  12.5 7.4 %copy-start.2 = (f32[2,512,128]{2,1,0:T(8,128)S(1)}, f32[2,512,128]{2,1,0:T(8,128)}, u32[]{:S(2)}) copy-start(f32[2,512,128]{2,1,0:T(8,128)} %param.7) | copy-start | bytes 1572868
  12.5 7.4 %copy-start.3 = (s32[2,512,128]{2,1,0:T(8,128)S(1)}, s32[2,512,128]{2,1,0:T(8,128)}, u32[]{:S(2)}) copy-start(s32[2,512,128]{2,1,0:T(8,128)} %param.9) | copy-start | bytes 1572868
  12.5 7.4 %copy-start.8 = (f32[2,512,128]{2,1,0:T(8,128)S(1)}, f32[2,512,128]{2,1,0:T(8,128)}, u32[]{:S(2)}) copy-start(f32[2,512,128]{2,1,0:T(8,128)} %param.11) | copy-start | bytes 1572868
  13.4 6.5 %copy-start = (s32[2,512,128]{2,1,0:T(8,128)S(1)}, s32[2,512,128]{2,1,0:T(8,128)}, u32[]{:S(2)}) copy-start(s32[2,512,128]{2,1,0:T(8,128)} %param.10) | copy-start | bytes 1572868
  13.5 2.7 %collective-permute-start.2 = (f32[2,512,25]{1,2,0:T(8,128)S(1)}, f32[2,512,25]{1,2,0:T(8,128)S(1)}, u32[]{:S(2)}, u32[]{:S(2)}) collective-permute-start(f32[2,512,25]{1,2,0:T(8,128)S(1)} %get-tuple-element.60), channel_id=1, source_target_pairs={{0,1},{1,2},{2,3},{4,5},{5,6},{6,7},{8,9},{9,10},{10,11},{12,13},{... | collective-permute-start | bytes 307208 | tf_op jit(solution)/shard_map/ppermute | solution.py:24
  14.9 5.0 %collective-permute-start.3 = (f32[2,512,25]{1,2,0:T(8,128)S(1)}, f32[2,512,25]{1,2,0:T(8,128)S(1)}, u32[]{:S(2)}, u32[]{:S(2)}) collective-permute-start(f32[2,512,25]{1,2,0:T(8,128)S(1)} %get-tuple-element.61), channel_id=1, source_target_pairs={{1,0},{2,1},{3,2},{5,4},{6,5},{7,6},{9,8},{10,9},{11,10},{13,12},{... | collective-permute-start | bytes 307208 | tf_op jit(solution)/shard_map/ppermute | solution.py:26
  22.5 6.1 %collective-permute-start.5 = (f32[2,25,128]{2,1,0:T(8,128)S(1)}, f32[2,25,128]{2,1,0:T(8,128)S(1)}, u32[]{:S(2)}, u32[]{:S(2)}) collective-permute-start(f32[2,25,128]{2,1,0:T(8,128)S(1)} %get-tuple-element.56), channel_id=1, source_target_pairs={{0,4},{1,5},{2,6},{3,7},{8,12},{9,13},{10,14},{11,15},{16,20},{17,... | collective-permute-start | bytes 76808 | tf_op jit(solution)/shard_map/ppermute | solution.py:24
  27.0 5.8 %collective-permute-start.6 = (f32[2,25,128]{2,1,0:T(8,128)S(1)}, f32[2,25,128]{2,1,0:T(8,128)S(1)}, u32[]{:S(2)}, u32[]{:S(2)}) collective-permute-start(f32[2,25,128]{2,1,0:T(8,128)S(1)} %get-tuple-element.57), channel_id=1, source_target_pairs={{4,0},{5,1},{6,2},{7,3},{12,8},{13,9},{14,10},{15,11},{20,16},{21,... | collective-permute-start | bytes 76808 | tf_op jit(solution)/shard_map/ppermute | solution.py:26
  33.8 6.7 %collective-permute-start.7 = (f32[2,512,25]{1,2,0:T(8,128)S(1)}, f32[2,512,25]{1,2,0:T(8,128)S(1)}, u32[]{:S(2)}, u32[]{:S(2)}) collective-permute-start(f32[2,512,25]{1,2,0:T(8,128)S(1)} %get-tuple-element.54), channel_id=1, source_target_pairs={{0,1},{1,2},{2,3},{4,5},{5,6},{6,7},{8,9},{9,10},{10,11},{12,13},{... | collective-permute-start | bytes 307208 | tf_op jit(solution)/shard_map/ppermute | solution.py:24
  37.8 4.0 %collective-permute-start.8 = (f32[2,512,25]{1,2,0:T(8,128)S(1)}, f32[2,512,25]{1,2,0:T(8,128)S(1)}, u32[]{:S(2)}, u32[]{:S(2)}) collective-permute-start(f32[2,512,25]{1,2,0:T(8,128)S(1)} %get-tuple-element.55), channel_id=1, source_target_pairs={{1,0},{2,1},{3,2},{5,4},{6,5},{7,6},{9,8},{10,9},{11,10},{13,12},{... | collective-permute-start | bytes 307208 | tf_op jit(solution)/shard_map/ppermute | solution.py:26
  39.2 12.8 %collective-permute-start.9 = (f32[1,512,128]{2,1,0:T(8,128)S(1)}, f32[1,512,128]{2,1,0:T(8,128)S(1)}, u32[]{:S(2)}, u32[]{:S(2)}) collective-permute-start(f32[1,512,128]{2,1,0:T(8,128)S(1)} %get-tuple-element.49), channel_id=1, source_target_pairs={{8,0},{16,8},{24,16},{9,1},{17,9},{25,17},{10,2},{18,10},{26,18},{... | collective-permute-start | bytes 786440 | tf_op jit(solution)/shard_map/ppermute | solution.py:36
  43.5 8.4 %copy-start.14 = (f32[2,512,128]{2,1,0:T(8,128)}, f32[2,512,128]{2,1,0:T(8,128)S(1)}, u32[]{:S(2)}) copy-start(f32[2,512,128]{2,1,0:T(8,128)S(1)} %get-tuple-element.66) | copy-start | bytes 1572868
  43.6 3.2 %collective-permute-start.10 = (f32[2,25,128]{2,1,0:T(8,128)S(1)}, f32[2,25,128]{2,1,0:T(8,128)S(1)}, u32[]{:S(2)}, u32[]{:S(2)}) collective-permute-start(f32[2,25,128]{2,1,0:T(8,128)S(1)} %get-tuple-element.52), channel_id=1, source_target_pairs={{0,4},{1,5},{2,6},{3,7},{8,12},{9,13},{10,14},{11,15},{16,20},{17,... | collective-permute-start | bytes 76808 | tf_op jit(solution)/shard_map/ppermute | solution.py:24
  45.2 5.8 %collective-permute-start.11 = (f32[2,25,128]{2,1,0:T(8,128)S(1)}, f32[2,25,128]{2,1,0:T(8,128)S(1)}, u32[]{:S(2)}, u32[]{:S(2)}) collective-permute-start(f32[2,25,128]{2,1,0:T(8,128)S(1)} %get-tuple-element.53), channel_id=1, source_target_pairs={{4,0},{5,1},{6,2},{7,3},{12,8},{13,9},{14,10},{15,11},{20,16},{21,... | collective-permute-start | bytes 76808 | tf_op jit(solution)/shard_map/ppermute | solution.py:26
  46.5 5.4 %copy-start.5 = (f32[2,512,128]{2,1,0:T(8,128)S(1)}, f32[2,512,128]{2,1,0:T(8,128)}, u32[]{:S(2)}) copy-start(f32[2,512,128]{2,1,0:T(8,128)} %param.13) | copy-start | bytes 1572868
  51.9 4.5 %copy-start.7 = (f32[2,512,128]{1,2,0:T(8,128)}, f32[2,512,128]{1,2,0:T(8,128)S(1)}, u32[]{:S(2)}) copy-start(f32[2,512,128]{1,2,0:T(8,128)S(1)} %convolution_bitcast_fusion.3) | copy-start | bytes 1572868
  52.9 37.1 %collective-permute-start.14 = (f32[1,512,128]{2,1,0:T(8,128)S(1)}, f32[1,512,128]{2,1,0:T(8,128)S(1)}, u32[]{:S(2)}, u32[]{:S(2)}) collective-permute-start(f32[1,512,128]{2,1,0:T(8,128)S(1)} %get-tuple-element.46), channel_id=1, source_target_pairs={{0,8},{8,16},{16,24},{1,9},{9,17},{17,25},{2,10},{10,18},{18,26},{... | collective-permute-start | bytes 786440 | tf_op jit(solution)/shard_map/ppermute | solution.py:36
  57.1 32.9 %collective-permute-start.12 = (f32[2,512,25]{1,2,0:T(8,128)}, f32[2,512,25]{1,2,0:T(8,128)}, u32[]{:S(2)}, u32[]{:S(2)}) collective-permute-start(f32[2,512,25]{1,2,0:T(8,128)} %get-tuple-element.50), channel_id=1, source_target_pairs={{0,1},{1,2},{2,3},{4,5},{5,6},{6,7},{8,9},{9,10},{10,11},{12,13},{... | collective-permute-start | bytes 307208 | tf_op jit(solution)/shard_map/ppermute | solution.py:24
  61.8 28.2 %collective-permute-start.13 = (f32[2,512,25]{1,2,0:T(8,128)}, f32[2,512,25]{1,2,0:T(8,128)}, u32[]{:S(2)}, u32[]{:S(2)}) collective-permute-start(f32[2,512,25]{1,2,0:T(8,128)} %get-tuple-element.51), channel_id=1, source_target_pairs={{1,0},{2,1},{3,2},{5,4},{6,5},{7,6},{9,8},{10,9},{11,10},{13,12},{... | collective-permute-start | bytes 307208 | tf_op jit(solution)/shard_map/ppermute | solution.py:26
  90.0 0.7 copy-start.10
  94.6 5.6 %collective-permute-start.15 = (f32[2,25,128]{2,1,0:T(8,128)S(1)}, f32[2,25,128]{2,1,0:T(8,128)S(1)}, u32[]{:S(2)}, u32[]{:S(2)}) collective-permute-start(f32[2,25,128]{2,1,0:T(8,128)S(1)} %get-tuple-element.44), channel_id=1, source_target_pairs={{0,4},{1,5},{2,6},{3,7},{8,12},{9,13},{10,14},{11,15},{16,20},{17,... | collective-permute-start | bytes 76808 | tf_op jit(solution)/shard_map/ppermute | solution.py:24
  98.6 5.8 %collective-permute-start.16 = (f32[2,25,128]{2,1,0:T(8,128)S(1)}, f32[2,25,128]{2,1,0:T(8,128)S(1)}, u32[]{:S(2)}, u32[]{:S(2)}) collective-permute-start(f32[2,25,128]{2,1,0:T(8,128)S(1)} %get-tuple-element.45), channel_id=1, source_target_pairs={{4,0},{5,1},{6,2},{7,3},{12,8},{13,9},{14,10},{15,11},{20,16},{21,... | collective-permute-start | bytes 76808 | tf_op jit(solution)/shard_map/ppermute | solution.py:26
  105.4 4.1 %collective-permute-start.17 = (f32[2,512,25]{1,2,0:T(8,128)S(1)}, f32[2,512,25]{1,2,0:T(8,128)S(1)}, u32[]{:S(2)}, u32[]{:S(2)}) collective-permute-start(f32[2,512,25]{1,2,0:T(8,128)S(1)} %get-tuple-element.42), channel_id=1, source_target_pairs={{0,1},{1,2},{2,3},{4,5},{5,6},{6,7},{8,9},{9,10},{10,11},{12,13},{... | collective-permute-start | bytes 307208 | tf_op jit(solution)/shard_map/ppermute | solution.py:24
  106.7 3.4 %copy-start.15 = (f32[2,512,128]{2,1,0:T(8,128)S(1)}, f32[2,512,128]{2,1,0:T(8,128)}, u32[]{:S(2)}) copy-start(f32[2,512,128]{2,1,0:T(8,128)} %copy-done.14) | copy-start | bytes 1572868
  106.7 3.4 %collective-permute-start.18 = (f32[2,512,25]{1,2,0:T(8,128)S(1)}, f32[2,512,25]{1,2,0:T(8,128)S(1)}, u32[]{:S(2)}, u32[]{:S(2)}) collective-permute-start(f32[2,512,25]{1,2,0:T(8,128)S(1)} %get-tuple-element.43), channel_id=1, source_target_pairs={{1,0},{2,1},{3,2},{5,4},{6,5},{7,6},{9,8},{10,9},{11,10},{13,12},{... | collective-permute-start | bytes 307208 | tf_op jit(solution)/shard_map/ppermute | solution.py:26
  108.2 12.0 %collective-permute-start.19 = (f32[1,512,128]{2,1,0:T(8,128)S(1)}, f32[1,512,128]{2,1,0:T(8,128)S(1)}, u32[]{:S(2)}, u32[]{:S(2)}) collective-permute-start(f32[1,512,128]{2,1,0:T(8,128)S(1)} %get-tuple-element.37), channel_id=1, source_target_pairs={{8,0},{16,8},{24,16},{9,1},{17,9},{25,17},{10,2},{18,10},{26,18},{... | collective-permute-start | bytes 786440 | tf_op jit(solution)/shard_map/ppermute | solution.py:36
  111.8 8.3 %copy-start.12 = (f32[2,512,128]{2,1,0:T(8,128)}, f32[2,512,128]{2,1,0:T(8,128)S(1)}, u32[]{:S(2)}) copy-start(f32[2,512,128]{2,1,0:T(8,128)S(1)} %get-tuple-element.69) | copy-start | bytes 1572868
  111.8 3.2 %collective-permute-start.20 = (f32[2,25,128]{2,1,0:T(8,128)S(1)}, f32[2,25,128]{2,1,0:T(8,128)S(1)}, u32[]{:S(2)}, u32[]{:S(2)}) collective-permute-start(f32[2,25,128]{2,1,0:T(8,128)S(1)} %get-tuple-element.40), channel_id=1, source_target_pairs={{0,4},{1,5},{2,6},{3,7},{8,12},{9,13},{10,14},{11,15},{16,20},{17,... | collective-permute-start | bytes 76808 | tf_op jit(solution)/shard_map/ppermute | solution.py:24
  113.4 5.8 %collective-permute-start.21 = (f32[2,25,128]{2,1,0:T(8,128)S(1)}, f32[2,25,128]{2,1,0:T(8,128)S(1)}, u32[]{:S(2)}, u32[]{:S(2)}) collective-permute-start(f32[2,25,128]{2,1,0:T(8,128)S(1)} %get-tuple-element.41), channel_id=1, source_target_pairs={{4,0},{5,1},{6,2},{7,3},{12,8},{13,9},{14,10},{15,11},{20,16},{21,... | collective-permute-start | bytes 76808 | tf_op jit(solution)/shard_map/ppermute | solution.py:26
  120.2 5.3 %copy-start.6 = (f32[2,512,128]{1,2,0:T(8,128)}, f32[2,512,128]{1,2,0:T(8,128)S(1)}, u32[]{:S(2)}) copy-start(f32[2,512,128]{1,2,0:T(8,128)S(1)} %convolution_bitcast_fusion.1) | copy-start | bytes 1572868
  121.1 36.0 %copy-start.4 = (s32[2,512,128]{2,1,0:T(8,128)S(1)}, s32[2,512,128]{2,1,0:T(8,128)}, u32[]{:S(2)}) copy-start(s32[2,512,128]{2,1,0:T(8,128)} %param.9) | copy-start | bytes 1572868
  121.1 35.3 %collective-permute-start.24 = (f32[1,512,128]{2,1,0:T(8,128)S(1)}, f32[1,512,128]{2,1,0:T(8,128)S(1)}, u32[]{:S(2)}, u32[]{:S(2)}) collective-permute-start(f32[1,512,128]{2,1,0:T(8,128)S(1)} %get-tuple-element.34), channel_id=1, source_target_pairs={{0,8},{8,16},{16,24},{1,9},{9,17},{17,25},{2,10},{10,18},{18,26},{... | collective-permute-start | bytes 786440 | tf_op jit(solution)/shard_map/ppermute | solution.py:36
  126.2 30.2 %collective-permute-start.22 = (f32[2,512,25]{1,2,0:T(8,128)}, f32[2,512,25]{1,2,0:T(8,128)}, u32[]{:S(2)}, u32[]{:S(2)}) collective-permute-start(f32[2,512,25]{1,2,0:T(8,128)} %get-tuple-element.38), channel_id=1, source_target_pairs={{0,1},{1,2},{2,3},{4,5},{5,6},{6,7},{8,9},{9,10},{10,11},{12,13},{... | collective-permute-start | bytes 307208 | tf_op jit(solution)/shard_map/ppermute | solution.py:24
  128.5 27.9 %collective-permute-start.23 = (f32[2,512,25]{1,2,0:T(8,128)}, f32[2,512,25]{1,2,0:T(8,128)}, u32[]{:S(2)}, u32[]{:S(2)}) collective-permute-start(f32[2,512,25]{1,2,0:T(8,128)} %get-tuple-element.39), channel_id=1, source_target_pairs={{1,0},{2,1},{3,2},{5,4},{6,5},{7,6},{9,8},{10,9},{11,10},{13,12},{... | collective-permute-start | bytes 307208 | tf_op jit(solution)/shard_map/ppermute | solution.py:26
  156.4 0.7 copy-start.9
  161.1 5.6 %collective-permute-start.25 = (f32[2,25,128]{2,1,0:T(8,128)S(1)}, f32[2,25,128]{2,1,0:T(8,128)S(1)}, u32[]{:S(2)}, u32[]{:S(2)}) collective-permute-start(f32[2,25,128]{2,1,0:T(8,128)S(1)} %get-tuple-element.32), channel_id=1, source_target_pairs={{0,4},{1,5},{2,6},{3,7},{8,12},{9,13},{10,14},{11,15},{16,20},{17,... | collective-permute-start | bytes 76808 | tf_op jit(solution)/shard_map/ppermute | solution.py:24
  165.1 5.8 %collective-permute-start.26 = (f32[2,25,128]{2,1,0:T(8,128)S(1)}, f32[2,25,128]{2,1,0:T(8,128)S(1)}, u32[]{:S(2)}, u32[]{:S(2)}) collective-permute-start(f32[2,25,128]{2,1,0:T(8,128)S(1)} %get-tuple-element.33), channel_id=1, source_target_pairs={{4,0},{5,1},{6,2},{7,3},{12,8},{13,9},{14,10},{15,11},{20,16},{21,... | collective-permute-start | bytes 76808 | tf_op jit(solution)/shard_map/ppermute | solution.py:26
  171.8 4.1 %collective-permute-start.27 = (f32[2,512,25]{1,2,0:T(8,128)S(1)}, f32[2,512,25]{1,2,0:T(8,128)S(1)}, u32[]{:S(2)}, u32[]{:S(2)}) collective-permute-start(f32[2,512,25]{1,2,0:T(8,128)S(1)} %get-tuple-element.30), channel_id=1, source_target_pairs={{0,1},{1,2},{2,3},{4,5},{5,6},{6,7},{8,9},{9,10},{10,11},{12,13},{... | collective-permute-start | bytes 307208 | tf_op jit(solution)/shard_map/ppermute | solution.py:24
  173.1 3.4 %copy-start.13 = (f32[2,512,128]{2,1,0:T(8,128)S(1)}, f32[2,512,128]{2,1,0:T(8,128)}, u32[]{:S(2)}) copy-start(f32[2,512,128]{2,1,0:T(8,128)} %copy-done.12) | copy-start | bytes 1572868
  173.1 3.4 %collective-permute-start.28 = (f32[2,512,25]{1,2,0:T(8,128)S(1)}, f32[2,512,25]{1,2,0:T(8,128)S(1)}, u32[]{:S(2)}, u32[]{:S(2)}) collective-permute-start(f32[2,512,25]{1,2,0:T(8,128)S(1)} %get-tuple-element.31), channel_id=1, source_target_pairs={{1,0},{2,1},{3,2},{5,4},{6,5},{7,6},{9,8},{10,9},{11,10},{13,12},{... | collective-permute-start | bytes 307208 | tf_op jit(solution)/shard_map/ppermute | solution.py:26
  174.6 10.9 %collective-permute-start.29 = (f32[1,512,128]{2,1,0:T(8,128)S(1)}, f32[1,512,128]{2,1,0:T(8,128)S(1)}, u32[]{:S(2)}, u32[]{:S(2)}) collective-permute-start(f32[1,512,128]{2,1,0:T(8,128)S(1)} %get-tuple-element.29), channel_id=1, source_target_pairs={{8,0},{16,8},{24,16},{9,1},{17,9},{25,17},{10,2},{18,10},{26,18},{... | collective-permute-start | bytes 786440 | tf_op jit(solution)/shard_map/ppermute | solution.py:36
